TPU v7x, 128 devices: a whole 4x4x4 slice. The times are simulated.
128 devices in a mesh: blk: 16 (over y, x_hi, core), rep: 8 (over x_lo, z).
Axes of the slice: x: 4 (x_hi: 2, x_lo: 2; x = x_hi * 2 + x_lo), y: 4, z: 4, core: 2. Of those that a mesh axis runs over, the one named last changes fastest.
Arguments:
- cotangent: bfloat16 [512, 256, 128], P('blk', 'rep'), may hold values from -6 to 6
- relu_mask: int32 [512, 256, 128], P('blk', 'rep'), may hold values 0 or 1
- aggregated: bfloat16 [512, 256, 128], P('blk', 'rep'), may hold values from -6 to 6
- weight: bfloat16 [256, 256], P('rep'), may hold values from -0.375 to 0.375
- tiles: bfloat16 [512, 16, 128, 128], P('blk'), may hold values from -0.125 to 0.125
- col_block: int32 [512, 16], P('blk'), may hold values from 0 to 511, as said below
- live_count: int32 [512], P('blk'), may hold values from 1 to 16, as said below
Outputs:
- input_grad: bfloat16 [512, 256, 128], P('blk', 'rep')
- weight_grad: float32 [256, 256], P('rep')
Inputs may be any that keep to these rules, and one draw needn't show every extreme that they name: The slab of a row block b is b // 32; the slab of col_block[b, s] lies at most 2 slabs from it around the closed cycle of the 16 slabs, and both distance 2 directions occur. `live_count`: row blocks of one slab share a density level, so live counts differ from slab to slab; some row block has all 16 slots live.
All inputs are finite; a program needn't handle non-finite values. No bound on the sum of `relu_mask` on one device may be relied on, other than what follows from the above.
Results may differ from a plain program's by a relative error of at most 0.0049.
Values may be sent and summed in bfloat16 or wider, within the bound.
A program may use at most 128 MiB of HBM per device.

v0:
```python
import math

import jax
import jax.numpy as jnp
from jax import lax
from jax.sharding import PartitionSpec as P

REACH = 2


def from_behind(value, axis, steps):
    count = lax.axis_size(axis)
    pairs = [(source, (source + steps) % count) for source in range(count)]
    return lax.ppermute(value, axis, pairs)


def on_device(cotangent, relu_mask, aggregated, weight, tiles, col_block, live_count):
    blocks_here = cotangent.shape[0]
    cols_here = cotangent.shape[1]
    tile_size = cotangent.shape[2]
    grad_z = cotangent * relu_mask.astype(jnp.bfloat16)
    gathered_part = lax.all_gather(grad_z, "rep", axis=1, tiled=True)
    grad_h = jnp.einsum("io,bon->bin", weight, gathered_part, preferred_element_type=jnp.float32)
    col_part = jnp.einsum(
        "bin,bon->io", aggregated, gathered_part, preferred_element_type=jnp.float32
    )
    grad_w = col_part
    grad_h, grad_w = (grad_h, grad_w)
    nodes_all = lax.axis_size("blk") * blocks_here * tile_size
    weight_grad = lax.psum(grad_w, "blk") * (1.0 / math.sqrt(nodes_all))
    grad_hb = grad_h.astype(jnp.bfloat16)
    slot_count = tiles.shape[1]
    slot_ids = jnp.arange(slot_count, dtype=jnp.int32)
    live = (slot_ids[None, :] < live_count[:, None]).astype(jnp.float32).reshape(-1)
    contrib = jnp.einsum("bkij,bfi->bkfj", tiles, grad_hb, preferred_element_type=jnp.float32)
    flat_terms = contrib.reshape(blocks_here * slot_count, cols_here * tile_size)
    targets = col_block.reshape(-1)
    slabs = lax.axis_size("blk")
    own_slab = lax.axis_index("blk")
    target_slab = targets // blocks_here
    window_slot = (target_slab - own_slab + REACH + slabs) % slabs
    position = window_slot * blocks_here + targets % blocks_here
    window_rows = (2 * REACH + 1) * blocks_here
    row_ids = jnp.arange(window_rows, dtype=jnp.int32)
    selector = (position[None, :] == row_ids[:, None]).astype(jnp.float32) * live[None, :]
    window = jnp.dot(
        selector, flat_terms, preferred_element_type=jnp.float32, precision=lax.Precision.HIGHEST
    )
    window = window.reshape(2 * REACH + 1, blocks_here, cols_here, tile_size)
    input_grad = window[REACH]
    upward = window[2 * REACH]
    downward = window[0]
    for step in range(REACH):
        upward = from_behind(upward, "blk", 1)
        downward = from_behind(downward, "blk", -1)
        if step + 1 < REACH:
            upward = upward + window[2 * REACH - step - 1]
            downward = downward + window[step + 1]
    input_grad = input_grad + upward + downward
    return (input_grad.astype(jnp.bfloat16), weight_grad)


def solution(mesh):
    placed = (
        P("blk", "rep", None),
        P("blk", "rep", None),
        P("blk", "rep", None),
        P("rep", None),
        P("blk", None, None, None),
        P("blk", None),
        P("blk"),
    )
    return jax.shard_map(
        on_device,
        mesh=mesh,
        in_specs=placed,
        out_specs=(P("blk", "rep", None), P("rep", None)),
        check_vma=False,
    )
```

profile of v0, /device:TPU:0, one launch (start us, length us, event | category | flops | bytes accessed | tf_op | source)
XLA Modules:
  0.0 174.0 jit_solution(14960853211397327882)
XLA Ops:
  7.2 1.9 %convert_multiply_fusion = bf16[32,32,128]{2,1,0:T(8,128)(2,1)} fusion(bf16[32,32,128]{2,1,0:T(8,128)(2,1)} %param.7, s32[32,32,128]{2,1,0:T(8,128)} %param.8), kind=kLoop, calls=%fused_computation.19 | loop fusion | flops 262144 | bytes 1048576 | tf_op jit(solution)/shard_map/mul | solution.py:21
  9.1 0.8 copy.9
  9.9 0.1 reshape.102
  10.0 0.7 fusion.13
  10.7 0.1 reshape.104
  10.8 43.8 %all-gather.2.cloned.1.call-done = bf16[32,256,128]{2,1,0:T(8,128)(2,1)} async-done(((bf16[32,32,128]{2,1,0:T(8,128)(2,1)}), bf16[32,256,128]{2,1,0:T(8,128)(2,1)}) %all-gather.2.cloned.1.call-update) | async-done | bytes 2097168 | tf_op jit(solution)/shard_map/all_gather | solution.py:22
  54.6 9.9 %fusion.4 = f32[32,32,16,128]{3,1,2,0:T(8,128)} fusion(bf16[32,16,128,128]{3,2,1,0:T(8,128)(2,1)} %param.11, bf16[32,256,128]{2,1,0:T(8,128)(2,1)} %all-gather.2.cloned.1.call-done, bf16[32,256]{1,0:T(8,128)(2,1)} %param.10), kind=kOutput, calls=%fused_computation.6 | convolution fusion | flops 604110848 | bytes 27279360 | tf_op jit(solution)/shard_map/bkij,bfi->bkfj/dot_general | solution.py:35
  64.5 11.3 %fusion = f32[160,4096]{1,0:T(8,128)S(1)} fusion(f32[64,8,32,128]{3,2,1,0:T(8,128)} %bitcast.46, f32[512]{0:T(512)S(1)} %reshape.104, s32[512]{0:T(512)S(1)} %fusion.18), kind=kOutput, calls=%fused_computation | convolution fusion | flops 4026695680 | bytes 11014144 | tf_op jit(solution)/shard_map/dot_general | solution.py:46
  75.9 0.2 slice_bitcast_fusion.4
  76.0 0.1 copy.13
  76.1 0.1 collective-permute-start
  76.2 0.1 copy.15
  76.3 5.4 %collective-permute-start.2 = (f32[32,32,128]{2,1,0:T(8,128)S(1)}, f32[32,32,128]{2,1,0:T(8,128)S(1)}, u32[]{:S(2)}, u32[]{:S(2)}) collective-permute-start(f32[32,32,128]{2,1,0:T(8,128)S(1)} %bitcast.47), channel_id=1, source_target_pairs={{0,120},{8,0},{16,8},{24,16},{32,24},{40,32},{48,40},{56,48},{64,5... | collective-permute-start | bytes 1572872 | tf_op jit(solution)/shard_map/ppermute | solution.py:14
  81.7 0.1 copy.16
  81.8 0.1 copy.14
  81.9 8.8 %collective-permute-done = f32[32,32,128]{2,1,0:T(8,128)S(1)} collective-permute-done((f32[32,32,128]{2,1,0:T(8,128)S(1)}, f32[32,32,128]{2,1,0:T(8,128)S(1)}, u32[]{:S(2)}, u32[]{:S(2)}) %collective-permute-start) | collective-permute-done | bytes 524320 | tf_op jit(solution)/shard_map/ppermute | solution.py:14
  90.8 0.1 bitcast_add_fusion.1
  91.0 0.1 bitcast_add_fusion
  91.0 5.4 %collective-permute-start.3 = (f32[32,32,128]{2,1,0:T(8,128)S(1)}, f32[32,32,128]{2,1,0:T(8,128)S(1)}, u32[]{:S(2)}, u32[]{:S(2)}) collective-permute-start(f32[32,32,128]{2,1,0:T(8,128)S(1)} %bitcast_add_fusion), channel_id=1, source_target_pairs={{0,120},{8,0},{16,8},{24,16},{32,24},{40,32},{48,40},{56,48},{64,5... | collective-permute-start | bytes 1572872 | tf_op jit(solution)/shard_map/ppermute | solution.py:14
  96.4 0.1 copy.12
  96.6 0.7 convolution_bitcast_fusion
  97.3 68.4 %psum.7 = f32[32,256]{1,0:T(8,128)S(1)} all-reduce(f32[32,256]{1,0:T(8,128)S(1)} %convolution_bitcast_fusion), channel_id=1, replica_groups=mesh['blk'=16,'rep'=8] {'blk'}, use_global_device_ids=true, to_apply=%region_0.0 | all-reduce | flops 8192 | bytes 65536 | tf_op jit(solution)/shard_map/psum | solution.py:30
  165.6 0.6 broadcast_multiply_fusion
  166.3 0.9 fusion.6
  (11 shorter events, 0.2 us)
Async XLA Ops:
  7.2 89.4 %copy-start = (bf16[32,32,128]{2,1,0:T(8,128)(2,1)S(1)}, bf16[32,32,128]{2,1,0:T(8,128)(2,1)}, u32[]{:S(2)}) copy-start(bf16[32,32,128]{2,1,0:T(8,128)(2,1)} %param.9) | copy-start | bytes 786436
  7.2 47.5 %all-gather.2.cloned.1.call-start = ((), (), s32[]{:S(2)}) async-start(), calls=%async_computation | async-start | bytes 2359296 | tf_op jit(solution)/shard_map/all_gather | solution.py:22
  76.1 14.6 %collective-permute-start = (f32[32,32,128]{2,1,0:T(8,128)S(1)}, f32[32,32,128]{2,1,0:T(8,128)S(1)}, u32[]{:S(2)}, u32[]{:S(2)}) collective-permute-start(f32[32,32,128]{2,1,0:T(8,128)S(1)} %bitcast.48), channel_id=1, source_target_pairs={{0,8},{8,16},{16,24},{24,32},{32,40},{40,48},{48,56},{56,64},{64,7... | collective-permute-start | bytes 1572872 | tf_op jit(solution)/shard_map/ppermute | solution.py:14
  76.3 14.6 %collective-permute-start.2 = (f32[32,32,128]{2,1,0:T(8,128)S(1)}, f32[32,32,128]{2,1,0:T(8,128)S(1)}, u32[]{:S(2)}, u32[]{:S(2)}) collective-permute-start(f32[32,32,128]{2,1,0:T(8,128)S(1)} %bitcast.47), channel_id=1, source_target_pairs={{0,120},{8,0},{16,8},{24,16},{32,24},{40,32},{48,40},{56,48},{64,5... | collective-permute-start | bytes 1572872 | tf_op jit(solution)/shard_map/ppermute | solution.py:14
  81.8 14.7 %copy-start.1 = (bf16[32,256,128]{2,1,0:T(8,128)(2,1)S(1)}, bf16[32,256,128]{2,1,0:T(8,128)(2,1)}, u32[]{:S(2)}) copy-start(bf16[32,256,128]{2,1,0:T(8,128)(2,1)} %all-gather.2.cloned.1.call-done) | copy-start | bytes 6291460
  90.9 75.4 %collective-permute-start.1 = (f32[32,32,128]{2,1,0:T(8,128)S(1)}, f32[32,32,128]{2,1,0:T(8,128)S(1)}, u32[]{:S(2)}, u32[]{:S(2)}) collective-permute-start(f32[32,32,128]{2,1,0:T(8,128)S(1)} %bitcast_add_fusion.1), channel_id=1, source_target_pairs={{0,8},{8,16},{16,24},{24,32},{32,40},{40,48},{48,56},{56,64},{64,7... | collective-permute-start | bytes 1572872 | tf_op jit(solution)/shard_map/ppermute | solution.py:14
  91.0 75.2 %collective-permute-start.3 = (f32[32,32,128]{2,1,0:T(8,128)S(1)}, f32[32,32,128]{2,1,0:T(8,128)S(1)}, u32[]{:S(2)}, u32[]{:S(2)}) collective-permute-start(f32[32,32,128]{2,1,0:T(8,128)S(1)} %bitcast_add_fusion), channel_id=1, source_target_pairs={{0,120},{8,0},{16,8},{24,16},{32,24},{40,32},{48,40},{56,48},{64,5... | collective-permute-start | bytes 1572872 | tf_op jit(solution)/shard_map/ppermute | solution.py:14
Sparse Core Ops, SparseCore 0:
  10.2 44.3 all-gather.1
where the time goes:
time: 174 us
  blocking collectives  68.4 us (39%)
  waiting for transfers between devices  52.7 us (30%)
  matrix products  21.9 us (13%)
  between operations  14.1 us (8%)
  starting transfers between devices  11 us (6%)
  other arithmetic  4.3 us (2%)
    psum x1, blocking collectives, on_device(): weight_grad = lax.psum(grad_w, 'blk') * (1.0 / math.sqrt(nodes_all))  68.4 us
    all_gather x1, waiting for transfers between devices, on_device(): gathered_part = lax.all_gather(grad_z, 'rep', axis=1, tiled=True)  43.8 us
    dot_general x1, matrix products, on_device(): jnp.dot(selector, flat_terms, preferred_element_type=jnp.float32, precisi...  11.3 us
    ppermute x4, starting transfers between devices, from_behind(): return lax.ppermute(value, axis, pairs)  11 us
    dot_general x1, matrix products, on_device(): jnp.einsum('bkij,bfi->bkfj', tiles, grad_hb, preferred_element_type=jnp.f...  9.9 us
    ppermute x4, waiting for transfers between devices, from_behind(): return lax.ppermute(value, axis, pairs)  8.83 us
  transfers between devices with their start and end apart: 5, of which 2 were waited for; matrix products, arithmetic and copies ran while one was open for 2% of the time, Pallas kernels for 0%

commit v1 on v0

v1 whole, which is shorter than its diff:
```python
import functools
import math

import jax
import jax.numpy as jnp
from jax import lax
from jax.experimental import pallas as pl
from jax.experimental.pallas import tpu as pltpu
from jax.sharding import PartitionSpec as P

REACH = 2
GROUPS = 4
PIECES = 4
MESH = pl.DeviceIdType.MESH
VMEM = pl.BlockSpec(memory_space=pltpu.VMEM)


def gather_kernel(
    ring, cot_ref, mask_ref, agg_ref, w_ref, gh_ref, wpart_ref, held, wacc, send_sem, recv_sem
):
    blocks, cols, _ = cot_ref.shape
    me = lax.axis_index("rep")
    side = me // ring
    place = me % ring

    def rank(xrel, zrel):
        x = side if xrel == 0 else 1 - side
        return x * ring + (place + zrel + ring) % ring

    to = {"x": rank(1, 0), "p": rank(0, 1), "m": rank(0, -1)}
    barrier = pltpu.get_barrier_semaphore()
    for name in ("x", "p", "m"):
        pl.semaphore_signal(barrier, inc=1, device_id={"rep": to[name]}, device_id_type=MESH)
    own = pl.multiple_of(me * cols, cols)
    held[:, pl.ds(own, cols), :] = cot_ref[...] * mask_ref[...].astype(jnp.bfloat16)
    wacc[...] = jnp.zeros_like(wacc)
    pl.semaphore_wait(barrier, 3)

    per = blocks // GROUPS

    def slot(xrel, zrel):
        return (xrel % 2) * ring + zrel % ring

    def copy(g, xrel, zrel, name, k):
        at = pl.multiple_of(rank(xrel, zrel) * cols, cols)
        piece = held.at[pl.ds(g * per, per), pl.ds(at, cols), :]
        there = {"x": (xrel + 1, zrel), "p": (xrel, zrel - 1), "m": (xrel, zrel + 1)}[name]
        return pltpu.make_async_remote_copy(
            src_ref=piece,
            dst_ref=piece,
            send_sem=send_sem.at[g, k],
            recv_sem=recv_sem.at[g, slot(*there)],
            device_id={"rep": to[name]},
            device_id_type=MESH,
        )

    def arrived(g, xrel, zrel):
        at = pl.multiple_of(rank(xrel, zrel) * cols, cols)
        piece = held.at[pl.ds(g * per, per), pl.ds(at, cols), :]
        pltpu.make_async_remote_copy(
            src_ref=piece,
            dst_ref=piece,
            send_sem=send_sem.at[g, 0],
            recv_sem=recv_sem.at[g, slot(xrel, zrel)],
            device_id={"rep": to["x"]},
            device_id_type=MESH,
        ).wait_recv()

    sent = []

    def send(*what):
        sent.append(copy(*what))
        sent[-1].start()

    for g in range(GROUPS):
        send(g, 0, 0, "x", 0)
        send(g, 0, 0, "p", 1)
        send(g, 0, 0, "m", 2)
    for g in range(GROUPS):
        arrived(g, 0, -1)
        arrived(g, 0, 1)
        arrived(g, 1, 0)
        if g % 2 == 0:
            send(g, 0, -1, "x", 3)
            send(g, 0, 1, "x", 4)
            send(g, 0, -1, "p", 5)
        else:
            send(g, 1, 0, "p", 3)
            send(g, 1, 0, "m", 4)
            send(g, 0, 1, "m", 5)
    for g in range(GROUPS):
        arrived(g, 1, -1)
        arrived(g, 1, 1)
        arrived(g, 0, 2)
        if g % 2 == 0:
            send(g, 1, -1, "p", 6)
        else:
            send(g, 1, 1, "m", 6)
    for g in range(GROUPS):
        arrived(g, 1, 2)

        def step(i, carry):
            for j in range(4):
                b = g * per + i * 4 + j
                z = held[b]
                gh_ref[b] = jnp.dot(
                    w_ref[...], z, preferred_element_type=jnp.float32
                ).astype(jnp.bfloat16)
                wacc[...] += lax.dot_general(
                    agg_ref[b], z, (((1,), (1,)), ((), ())), preferred_element_type=jnp.float32
                )
            return carry

        lax.fori_loop(0, per // 4, step, 0)
    wpart_ref[...] = wacc[...]
    for one in sent:
        one.wait_send()


def tile_kernel(slabs, blocks, col_ref, live_ref, gh_ref, tiles_ref, mid_ref, out_ref, acc):
    step = pl.program_id(0)
    per, slots = tiles_ref.shape[0], tiles_ref.shape[1]
    window = (2 * REACH + 1) * blocks
    slab = lax.axis_index("blk")

    @pl.when(step == 0)
    def _():
        acc[...] = jnp.zeros_like(acc)

    for k in range(per):
        b = step * per + k
        live = live_ref[b]
        grad = gh_ref[b]
        for first in range(0, slots, 4):

            @pl.when(first < live)
            def _(first=first, k=k, b=b, live=live, grad=grad):
                for s in range(first, first + 4):
                    col = col_ref[b, s]
                    away = (col // blocks - slab + (REACH + slabs)) % slabs
                    row = jnp.where(s < live, away * blocks + col % blocks, window)
                    term = jnp.dot(grad, tiles_ref[k, s], preferred_element_type=jnp.float32)
                    acc[row] += term

    @pl.when(step == pl.num_programs(0) - 1)
    def _():
        for w in range(2 * REACH + 1):
            part = acc[w * blocks : (w + 1) * blocks]
            if w == REACH:
                mid_ref[...] = part
            else:
                out_ref[w - (w > REACH)] = part.astype(jnp.bfloat16)


def exchange_kernel(
    slabs, scale, mid_ref, out_ref, wpart_ref, ig_ref, wg_ref,
    near_in, far_in, both, both_in, far_here, wsum, wsum_in, sems_s, sems_r,
):
    blocks = mid_ref.shape[0]
    per = blocks // PIECES
    me = lax.axis_index("blk")
    core = me % 2
    ahead = 2 * core - 1

    def at(offset):
        return (me + offset + slabs) % slabs

    def across(bit):
        return me + bit - 2 * bit * ((me // bit) % 2)

    bits = [1] + [bit for bit in (4, 8) if bit < slabs] + [2]
    partner = across(1)
    peers = [at(ahead), at(2 * ahead), at(-2 * ahead)] + [across(bit) for bit in bits]
    barrier = pltpu.get_barrier_semaphore()
    for peer in peers:
        pl.semaphore_signal(barrier, inc=1, device_id={"blk": peer}, device_id_type=MESH)
    pl.semaphore_wait(barrier, len(peers))

    far, near = 3 * core, 1 + core
    back_far, back_near = 3 - 3 * core, 2 - core

    def copy(src, dst, k, peer):
        return pltpu.make_async_remote_copy(
            src_ref=src,
            dst_ref=dst,
            send_sem=sems_s.at[k],
            recv_sem=sems_r.at[k],
            device_id={"blk": peer},
            device_id_type=MESH,
        )

    cuts = [pl.ds(p * per, per) for p in range(PIECES)]
    helps = [copy(out_ref.at[back_far, c], far_here.at[c], p, partner) for p, c in enumerate(cuts)]
    k = PIECES
    summed = [copy(both.at[c], both_in.at[c], k + p, at(ahead)) for p, c in enumerate(cuts)]
    k += PIECES
    far_copy = copy(out_ref.at[far], far_in, k, at(2 * ahead))
    near_copy = copy(out_ref.at[back_near], near_in, k + 1, partner)
    k += 2
    for one in helps:
        one.start()
    far_copy.start()
    near_copy.start()
    weights = []
    for i, bit in enumerate(bits):
        src = wpart_ref if i == 0 else wsum.at[i - 1]
        weights.append(copy(src, wsum_in.at[i], k + i, across(bit)))
    weights[0].start()
    for p, c in enumerate(cuts):
        helps[p].wait_recv()
        both[c] = (
            out_ref[near, c].astype(jnp.float32) + far_here[c].astype(jnp.float32)
        ).astype(jnp.bfloat16)
        summed[p].start()
    for i in range(len(bits)):
        weights[i].wait_recv()
        total = (wpart_ref[...] if i == 0 else wsum[i - 1]) + wsum_in[i]
        if i + 1 < len(bits):
            wsum[i] = total
            weights[i + 1].start()
        else:
            wg_ref[...] = total * scale
    near_copy.wait_recv()
    far_copy.wait_recv()
    for p, c in enumerate(cuts):
        summed[p].wait_recv()
        ig_ref[c] = (
            mid_ref[c]
            + near_in[c].astype(jnp.float32)
            + far_in[c].astype(jnp.float32)
            + both_in[c].astype(jnp.float32)
        ).astype(jnp.bfloat16)
    for one in helps + summed + weights + [far_copy, near_copy]:
        one.wait_send()


def on_device(cotangent, relu_mask, aggregated, weight, tiles, col_block, live_count):
    blocks, cols, size = cotangent.shape
    slots = tiles.shape[1]
    slabs, reps = lax.axis_size("blk"), lax.axis_size("rep")
    width = weight.shape[1]
    ring = reps // 2
    bf16, f32 = jnp.bfloat16, jnp.float32
    dma = pltpu.SemaphoreType.DMA

    grad_h, wpart = pl.pallas_call(
        functools.partial(gather_kernel, ring),
        out_shape=(
            jax.ShapeDtypeStruct((blocks, cols, size), bf16),
            jax.ShapeDtypeStruct((cols, width), f32),
        ),
        in_specs=[VMEM] * 4,
        out_specs=(VMEM, VMEM),
        scratch_shapes=[
            pltpu.VMEM((blocks, width, size), bf16),
            pltpu.VMEM((cols, width), f32),
            dma((GROUPS, 7)),
            dma((GROUPS, reps)),
        ],
        compiler_params=pltpu.CompilerParams(
            collective_id=0, has_side_effects=True, vmem_limit_bytes=32 << 20
        ),
        name="gather",
    )(cotangent, relu_mask, aggregated, weight)

    per = 2
    middle, outer = pl.pallas_call(
        functools.partial(tile_kernel, slabs, blocks),
        out_shape=(
            jax.ShapeDtypeStruct((blocks, cols, size), f32),
            jax.ShapeDtypeStruct((2 * REACH, blocks, cols, size), bf16),
        ),
        grid_spec=pltpu.PrefetchScalarGridSpec(
            num_scalar_prefetch=2,
            grid=(blocks // per,),
            in_specs=[
                pl.BlockSpec((blocks, cols, size), lambda i, c, n: (0, 0, 0)),
                pl.BlockSpec((per, slots, size, size), lambda i, c, n: (i, 0, 0, 0)),
            ],
            out_specs=[
                pl.BlockSpec((blocks, cols, size), lambda i, c, n: (0, 0, 0)),
                pl.BlockSpec((2 * REACH, blocks, cols, size), lambda i, c, n: (0, 0, 0, 0)),
            ],
            scratch_shapes=[pltpu.VMEM(((2 * REACH + 1) * blocks + 1, cols, size), f32)],
        ),
        compiler_params=pltpu.CompilerParams(
            dimension_semantics=("arbitrary",), vmem_limit_bytes=32 << 20
        ),
        name="tiles",
    )(col_block, live_count, grad_h, tiles)

    scale = 1.0 / math.sqrt(slabs * blocks * size)
    levels = slabs.bit_length() - 1
    held = pltpu.VMEM((blocks, cols, size), bf16)
    count = 2 * PIECES + 2 + levels
    return pl.pallas_call(
        functools.partial(exchange_kernel, slabs, scale),
        out_shape=(
            jax.ShapeDtypeStruct((blocks, cols, size), bf16),
            jax.ShapeDtypeStruct((cols, width), f32),
        ),
        in_specs=[VMEM] * 3,
        out_specs=(VMEM, VMEM),
        scratch_shapes=[
            held, held, held, held, held,
            pltpu.VMEM((levels, cols, width), f32),
            pltpu.VMEM((levels, cols, width), f32),
            dma((count,)),
            dma((count,)),
        ],
        compiler_params=pltpu.CompilerParams(
            collective_id=1, has_side_effects=True, vmem_limit_bytes=32 << 20
        ),
        name="exchange",
    )(middle, outer, wpart)


def solution(mesh):
    placed = (
        P("blk", "rep", None),
        P("blk", "rep", None),
        P("blk", "rep", None),
        P("rep", None),
        P("blk", None, None, None),
        P("blk", None),
        P("blk"),
    )
    return jax.shard_map(
        on_device,
        mesh=mesh,
        in_specs=placed,
        out_specs=(P("blk", "rep", None), P("rep", None)),
        check_vma=False,
    )
```

time: 174 us -> 69.7 us (0.40)
  the two profiles are of different devices: /device:TPU:0 before, /device:TPU:1 now
where the time goes in v1:
time: 69.7 us; the launch traced here: 69.3 us
  Pallas kernels  56.5 us (81%)
  local copies, waits for them, and re-layouts  12.2 us (18%)
    pallas_call x1, Pallas kernels, on_device(): pl.pallas_call(functools.partial(gather_kernel, ring), out_shape=(jax.Sha...  21.5 us
    pallas_call x1, Pallas kernels, on_device(): pl.pallas_call(functools.partial(exchange_kernel, slabs, scale), out_shap...  20.5 us
    pallas_call x1, Pallas kernels, on_device(): pl.pallas_call(functools.partial(tile_kernel, slabs, blocks), out_shape=(...  14.5 us
    unnamed x15, local copies, waits for them, and re-layouts  12.2 us

profile of v1, /device:TPU:1, one launch (start us, length us, event | category | flops | bytes accessed | tf_op | source)
XLA Modules:
  0.0 69.3 jit_solution(14483241525046059637)
XLA Ops:
  0.6 0.8 %copy.9.col_ref = s32[32,16]{1,0:T(8,128)S(1)} copy(s32[32,16]{0,1:T(8,128)} %param.12) | data formatting | bytes 4096 | tf_op args[5]
  1.4 0.0 copy-start.1
  1.4 1.0 %copy-done.1 = s32[32,32,128]{2,1,0:T(8,128)S(1)} copy-done((s32[32,32,128]{2,1,0:T(8,128)S(1)}, s32[32,32,128]{2,1,0:T(8,128)}, u32[]{:S(2)}) %copy-start.1) | copy-done | bytes 524312
  2.4 0.0 copy-start.2
  2.4 0.9 %copy-done.2 = bf16[32,32,128]{2,1,0:T(8,128)(2,1)S(1)} copy-done((bf16[32,32,128]{2,1,0:T(8,128)(2,1)S(1)}, bf16[32,32,128]{2,1,0:T(8,128)(2,1)}, u32[]{:S(2)}) %copy-start.2) | copy-done | bytes 262168
  3.4 0.0 copy-start.3
  3.4 0.9 %copy-done.3 = bf16[32,32,128]{2,1,0:T(8,128)(2,1)S(1)} copy-done((bf16[32,32,128]{2,1,0:T(8,128)(2,1)S(1)}, bf16[32,32,128]{2,1,0:T(8,128)(2,1)}, u32[]{:S(2)}) %copy-start.3) | copy-done | bytes 262168
  4.3 0.0 copy-start.4
  4.3 0.7 %copy-done.4 = bf16[32,256]{1,0:T(8,128)(2,1)S(1)} copy-done((bf16[32,256]{1,0:T(8,128)(2,1)S(1)}, bf16[32,256]{1,0:T(8,128)(2,1)}, u32[]{:S(2)}) %copy-start.4) | copy-done | bytes 16408
  5.1 21.5 %gather.1 = (bf16[32,32,128]{2,1,0:T(8,128)(2,1)S(1)}, f32[32,256]{1,0:T(8,128)S(1)}) custom-call(bf16[32,32,128]{2,1,0:T(8,128)(2,1)S(1)} %copy-done.2, s32[32,32,128]{2,1,0:T(8,128)S(1)} %copy-done.1, bf16[32,32,128]{2,1,0:T(8,128)(2,1)S(1)} %copy-done.3, bf16[32,256]{1,0:T(8,128)(2,1)S(1)} %copy-done.4), custom_call_target="tpu_custom_call" | custom-call | tf_op jit(solution)/shard_map/gather/pallas_call | solution.py:246
  26.6 0.0 copy-start
  26.6 5.8 %copy-done = bf16[32,16,128,128]{3,2,1,0:T(8,128)(2,1)S(1)} copy-done((bf16[32,16,128,128]{3,2,1,0:T(8,128)(2,1)S(1)}, bf16[32,16,128,128]{3,2,1,0:T(8,128)(2,1)}, u32[]{:S(2)}) %copy-start) | copy-done | bytes 16777240
  32.3 0.0 copy-start.5
  32.3 0.7 copy-done.5
  33.0 14.5 %tiles.1 = (f32[32,32,128]{2,1,0:T(8,128)S(1)}, bf16[4,32,32,128]{3,2,1,0:T(8,128)(2,1)S(1)}) custom-call(s32[32,16]{1,0:T(8,128)S(1)} %copy.9.col_ref, s32[32]{0:T(128)S(1)} %copy-done.5, bf16[32,32,128]{2,1,0:T(8,128)(2,1)S(1)} %get-tuple-element.6.gh_ref, bf16[32,16,128,128]{3,2,1,0:T(8,128)(2,1)S(1)} %copy-done), custom_call_target="tpu_custom_call" | custom-call | tf_op jit(solution)/shard_map/tiles/pallas_call | solution.py:267
  47.5 20.5 %exchange.1 = (bf16[32,32,128]{2,1,0:T(8,128)(2,1)S(1)}, f32[32,256]{1,0:T(8,128)S(1)}) custom-call(f32[32,32,128]{2,1,0:T(8,128)S(1)} %get-tuple-element.7.mid_ref, bf16[4,32,32,128]{3,2,1,0:T(8,128)(2,1)S(1)} %get-tuple-element.8.out_ref, f32[32,256]{1,0:T(8,128)S(1)} %get-tuple-element.9.wpart_ref), custom_call_target="tpu_custom_call" | custom-call | tf_op jit(solution)/shard_map/exchange/pallas_call | solution.py:296
  68.0 0.7 %copy.12 = bf16[32,32,128]{2,1,0:T(8,128)(2,1)} copy(bf16[32,32,128]{2,1,0:T(8,128)(2,1)S(1)} %get-tuple-element.12) | data formatting | bytes 524288
  68.7 0.6 copy.13
Async XLA Ops:
  1.4 1.0 %copy-start.1 = (s32[32,32,128]{2,1,0:T(8,128)S(1)}, s32[32,32,128]{2,1,0:T(8,128)}, u32[]{:S(2)}) copy-start(s32[32,32,128]{2,1,0:T(8,128)} %mask_ref.1) | copy-start | bytes 1572868
  2.4 0.9 %copy-start.2 = (bf16[32,32,128]{2,1,0:T(8,128)(2,1)S(1)}, bf16[32,32,128]{2,1,0:T(8,128)(2,1)}, u32[]{:S(2)}) copy-start(bf16[32,32,128]{2,1,0:T(8,128)(2,1)} %cot_ref.1) | copy-start | bytes 786436
  3.4 0.9 %copy-start.3 = (bf16[32,32,128]{2,1,0:T(8,128)(2,1)S(1)}, bf16[32,32,128]{2,1,0:T(8,128)(2,1)}, u32[]{:S(2)}) copy-start(bf16[32,32,128]{2,1,0:T(8,128)(2,1)} %agg_ref.1) | copy-start | bytes 786436
  4.3 0.7 %copy-start.4 = (bf16[32,256]{1,0:T(8,128)(2,1)S(1)}, bf16[32,256]{1,0:T(8,128)(2,1)}, u32[]{:S(2)}) copy-start(bf16[32,256]{1,0:T(8,128)(2,1)} %w_ref.1) | copy-start | bytes 49156
  26.6 5.8 %copy-start = (bf16[32,16,128,128]{3,2,1,0:T(8,128)(2,1)S(1)}, bf16[32,16,128,128]{3,2,1,0:T(8,128)(2,1)}, u32[]{:S(2)}) copy-start(bf16[32,16,128,128]{3,2,1,0:T(8,128)(2,1)} %tiles_ref.1) | copy-start | bytes 50331652
  32.3 0.7 copy-start.5

commit v2 on v1

--- a/solution.py
+++ b/solution.py
@@ -13,12 +13,20 @@
 PIECES = 4
 MESH = pl.DeviceIdType.MESH
 VMEM = pl.BlockSpec(memory_space=pltpu.VMEM)
+SMEM = pl.BlockSpec(memory_space=pltpu.SMEM)
+HBM = pl.BlockSpec(memory_space=pltpu.HBM)
 
 
 def gather_kernel(
-    ring, cot_ref, mask_ref, agg_ref, w_ref, gh_ref, wpart_ref, held, wacc, send_sem, recv_sem
+    ring, cot_hbm, mask_hbm, agg_hbm, w_hbm, tiles_hbm, gh_ref, wpart_ref, tiles_ref,
+    cot_ref, mask_ref, agg_ref, w_ref, held, wacc, load_sem, send_sem, recv_sem,
 ):
     blocks, cols, _ = cot_ref.shape
+    pairs = ((mask_hbm, mask_ref), (cot_hbm, cot_ref), (agg_hbm, agg_ref), (w_hbm, w_ref))
+    pairs += ((tiles_hbm, tiles_ref),)
+    loads = [pltpu.make_async_copy(a, b, load_sem.at[i]) for i, (a, b) in enumerate(pairs)]
+    for one in loads[:4]:
+        one.start()
     me = lax.axis_index("rep")
     side = me // ring
     place = me % ring
@@ -32,6 +40,8 @@
     for name in ("x", "p", "m"):
         pl.semaphore_signal(barrier, inc=1, device_id={"rep": to[name]}, device_id_type=MESH)
     own = pl.multiple_of(me * cols, cols)
+    loads[0].wait()
+    loads[1].wait()
     held[:, pl.ds(own, cols), :] = cot_ref[...] * mask_ref[...].astype(jnp.bfloat16)
     wacc[...] = jnp.zeros_like(wacc)
     pl.semaphore_wait(barrier, 3)
@@ -76,6 +86,9 @@
         send(g, 0, 0, "x", 0)
         send(g, 0, 0, "p", 1)
         send(g, 0, 0, "m", 2)
+    loads[4].start()
+    loads[2].wait()
+    loads[3].wait()
     for g in range(GROUPS):
         arrived(g, 0, -1)
         arrived(g, 0, 1)
@@ -115,41 +128,42 @@
     wpart_ref[...] = wacc[...]
     for one in sent:
         one.wait_send()
+    loads[4].wait()
 
 
 def tile_kernel(slabs, blocks, col_ref, live_ref, gh_ref, tiles_ref, mid_ref, out_ref, acc):
-    step = pl.program_id(0)
-    per, slots = tiles_ref.shape[0], tiles_ref.shape[1]
+    slots = tiles_ref.shape[1]
     window = (2 * REACH + 1) * blocks
-    slab = lax.axis_index("blk")
-
-    @pl.when(step == 0)
-    def _():
-        acc[...] = jnp.zeros_like(acc)
-
-    for k in range(per):
-        b = step * per + k
-        live = live_ref[b]
-        grad = gh_ref[b]
-        for first in range(0, slots, 4):
-
-            @pl.when(first < live)
-            def _(first=first, k=k, b=b, live=live, grad=grad):
-                for s in range(first, first + 4):
-                    col = col_ref[b, s]
-                    away = (col // blocks - slab + (REACH + slabs)) % slabs
-                    row = jnp.where(s < live, away * blocks + col % blocks, window)
-                    term = jnp.dot(grad, tiles_ref[k, s], preferred_element_type=jnp.float32)
-                    acc[row] += term
-
-    @pl.when(step == pl.num_programs(0) - 1)
-    def _():
-        for w in range(2 * REACH + 1):
-            part = acc[w * blocks : (w + 1) * blocks]
-            if w == REACH:
-                mid_ref[...] = part
-            else:
-                out_ref[w - (w > REACH)] = part.astype(jnp.bfloat16)
+    every = slabs * blocks
+    first_row = (lax.axis_index("blk") - REACH) * blocks
+    acc[...] = jnp.zeros_like(acc)
+
+    def step(i, carry):
+        pair = (2 * i, 2 * i + 1)
+        live = [live_ref[b] for b in pair]
+        most = jnp.maximum(live[0], live[1])
+        for half in range(2):
+
+            @pl.when(half * (slots // 2) < most)
+            def _(half=half):
+                for k, b in enumerate(pair):
+                    grad = gh_ref[b]
+                    for s in range(half * (slots // 2), (half + 1) * (slots // 2)):
+                        away = (col_ref[s, b] - first_row + every) & (every - 1)
+                        row = jnp.where(s < live[k], away, window)
+                        acc[row] += jnp.dot(
+                            grad, tiles_ref[b, s], preferred_element_type=jnp.float32
+                        )
+
+        return carry
+
+    lax.fori_loop(0, blocks // 2, step, 0)
+    for w in range(2 * REACH + 1):
+        part = acc[w * blocks : (w + 1) * blocks]
+        if w == REACH:
+            mid_ref[...] = part
+        else:
+            out_ref[w - (w > REACH)] = part.astype(jnp.bfloat16)
 
 
 def exchange_kernel(
@@ -243,17 +257,23 @@
     bf16, f32 = jnp.bfloat16, jnp.float32
     dma = pltpu.SemaphoreType.DMA
 
-    grad_h, wpart = pl.pallas_call(
+    grad_h, wpart, tiles_here = pl.pallas_call(
         functools.partial(gather_kernel, ring),
         out_shape=(
             jax.ShapeDtypeStruct((blocks, cols, size), bf16),
             jax.ShapeDtypeStruct((cols, width), f32),
-        ),
-        in_specs=[VMEM] * 4,
-        out_specs=(VMEM, VMEM),
+            jax.ShapeDtypeStruct(tiles.shape, bf16),
+        ),
+        in_specs=[HBM] * 5,
+        out_specs=(VMEM, VMEM, VMEM),
         scratch_shapes=[
+            pltpu.VMEM((blocks, cols, size), bf16),
+            pltpu.VMEM((blocks, cols, size), jnp.int32),
+            pltpu.VMEM((blocks, cols, size), bf16),
+            pltpu.VMEM((cols, width), bf16),
             pltpu.VMEM((blocks, width, size), bf16),
             pltpu.VMEM((cols, width), f32),
+            dma((5,)),
             dma((GROUPS, 7)),
             dma((GROUPS, reps)),
         ],
@@ -261,33 +281,20 @@
             collective_id=0, has_side_effects=True, vmem_limit_bytes=32 << 20
         ),
         name="gather",
-    )(cotangent, relu_mask, aggregated, weight)
-
-    per = 2
+    )(*[pltpu.with_memory_space_constraint(a, pltpu.HBM) for a in (cotangent, relu_mask, aggregated, weight)], tiles)
+
     middle, outer = pl.pallas_call(
         functools.partial(tile_kernel, slabs, blocks),
         out_shape=(
             jax.ShapeDtypeStruct((blocks, cols, size), f32),
             jax.ShapeDtypeStruct((2 * REACH, blocks, cols, size), bf16),
         ),
-        grid_spec=pltpu.PrefetchScalarGridSpec(
-            num_scalar_prefetch=2,
-            grid=(blocks // per,),
-            in_specs=[
-                pl.BlockSpec((blocks, cols, size), lambda i, c, n: (0, 0, 0)),
-                pl.BlockSpec((per, slots, size, size), lambda i, c, n: (i, 0, 0, 0)),
-            ],
-            out_specs=[
-                pl.BlockSpec((blocks, cols, size), lambda i, c, n: (0, 0, 0)),
-                pl.BlockSpec((2 * REACH, blocks, cols, size), lambda i, c, n: (0, 0, 0, 0)),
-            ],
-            scratch_shapes=[pltpu.VMEM(((2 * REACH + 1) * blocks + 1, cols, size), f32)],
-        ),
-        compiler_params=pltpu.CompilerParams(
-            dimension_semantics=("arbitrary",), vmem_limit_bytes=32 << 20
-        ),
+        in_specs=[SMEM, SMEM, VMEM, VMEM],
+        out_specs=(VMEM, VMEM),
+        scratch_shapes=[pltpu.VMEM(((2 * REACH + 1) * blocks + 1, cols, size), f32)],
+        compiler_params=pltpu.CompilerParams(vmem_limit_bytes=12 << 20),
         name="tiles",
-    )(col_block, live_count, grad_h, tiles)
+    )(col_block.T, live_count, grad_h, tiles_here)
 
     scale = 1.0 / math.sqrt(slabs * blocks * size)
     levels = slabs.bit_length() - 1

time: 69.7 us -> 51.3 us (0.74)
  local copies, waits for them, and re-layouts: 12.2 us -> 1.33 us
  Pallas kernels: 56.5 us -> 49.1 us
    unnamed x15 -> x6, local copies, waits for them, and re-layouts: 12.2 us -> 1.33 us
    pallas_call x1, Pallas kernels: 14.5 us -> 9.25 us  [on_device(): pl.pallas_call(functools.partial(tile_kernel, slabs, blocks), out_shape=(...]
    pallas_call x1, Pallas kernels: 20.5 us -> 17.8 us  [on_device(): pl.pallas_call(functools.partial(exchange_kernel, slabs, scale), out_shap...]
where the time goes in v2:
time: 51.3 us; the launch traced here: 51.1 us
  Pallas kernels  49.1 us (96%)
  local copies, waits for them, and re-layouts  1.33 us (3%)
  between operations  0.68 us (1%)
    pallas_call x1, Pallas kernels, on_device(): pl.pallas_call(functools.partial(gather_kernel, ring), out_shape=(jax.Sha...  22 us
    pallas_call x1, Pallas kernels, on_device(): pl.pallas_call(functools.partial(exchange_kernel, slabs, scale), out_shap...  17.8 us
    pallas_call x1, Pallas kernels, on_device(): pl.pallas_call(functools.partial(tile_kernel, slabs, blocks), out_shape=(...  9.25 us
    unnamed x6, local copies, waits for them, and re-layouts  1.33 us

profile of v2, /device:TPU:1, one launch (start us, length us, event | category | flops | bytes accessed | tf_op | source)
XLA Modules:
  0.0 51.1 jit_solution(1814540030523641952)
XLA Ops:
  0.6 0.0 copy-start.1
  0.6 0.0 copy-start
  0.7 22.0 %gather.1 = (bf16[32,32,128]{2,1,0:T(8,128)(2,1)S(1)}, f32[32,256]{1,0:T(8,128)S(1)}, bf16[32,16,128,128]{3,2,1,0:T(8,128)(2,1)S(1)}) custom-call(bf16[32,32,128]{2,1,0:T(8,128)(2,1)} %cot_hbm.1, s32[32,32,128]{2,1,0:T(8,128)} %mask_hbm.1, bf16[32,32,128]{2,1,0:T(8,128)(2,1)} %agg_hbm.1, bf16[32,256]{1,0:T(8,128)(2,1)} %w_hbm.1, ...), custom_call_target="tpu_custom_call" | custom-call | tf_op jit(solution)/shard_map/gather/pallas_call | solution.py:260
  22.7 0.0 copy-done.1
  22.7 0.0 copy-done
  22.7 9.2 %tiles.1 = (f32[32,32,128]{2,1,0:T(8,128)S(1)}, bf16[4,32,32,128]{3,2,1,0:T(8,128)(2,1)S(1)}) custom-call(s32[16,32]{1,0:T(8,128)S(1)} %bitcast.1, s32[32]{0:T(128)S(1)} %copy-done.1, bf16[32,32,128]{2,1,0:T(8,128)(2,1)S(1)} %get-tuple-element.7.gh_ref, bf16[32,16,128,128]{3,2,1,0:T(8,128)(2,1)S(1)} %get-tuple-element.8.tiles_ref), custom_call_target="tpu_custom_call" | custom-call | tf_op jit(solution)/shard_map/tiles/pallas_call | solution.py:286
  31.9 17.8 %exchange.1 = (bf16[32,32,128]{2,1,0:T(8,128)(2,1)S(1)}, f32[32,256]{1,0:T(8,128)S(1)}) custom-call(f32[32,32,128]{2,1,0:T(8,128)S(1)} %get-tuple-element.9.mid_ref, bf16[4,32,32,128]{3,2,1,0:T(8,128)(2,1)S(1)} %get-tuple-element.10.out_ref, f32[32,256]{1,0:T(8,128)S(1)} %get-tuple-element.11.wpart_ref), custom_call_target="tpu_custom_call" | custom-call | tf_op jit(solution)/shard_map/exchange/pallas_call | solution.py:303
  49.7 0.7 %copy.11 = bf16[32,32,128]{2,1,0:T(8,128)(2,1)} copy(bf16[32,32,128]{2,1,0:T(8,128)(2,1)S(1)} %get-tuple-element.14) | data formatting | bytes 524288
  50.5 0.6 %copy.12 = f32[32,256]{1,0:T(8,128)} copy(f32[32,256]{1,0:T(8,128)S(1)} %get-tuple-element.15) | data formatting | bytes 65536
Async XLA Ops:
  0.6 22.0 %copy-start.1 = (s32[32]{0:T(128)S(1)}, s32[32]{0:T(128)}, u32[]{:S(2)}) copy-start(s32[32]{0:T(128)} %live_ref.1) | copy-start | bytes 388
  0.6 22.0 %copy-start = (s32[32,16]{0,1:T(8,128)S(1)}, s32[32,16]{0,1:T(8,128)}, u32[]{:S(2)}) copy-start(s32[32,16]{0,1:T(8,128)} %param.12) | copy-start | bytes 6148

commit v3 on v2

--- a/solution.py
+++ b/solution.py
@@ -9,7 +9,7 @@
 from jax.sharding import PartitionSpec as P
 
 REACH = 2
-GROUPS = 4
+GROUPS = 8
 PIECES = 4
 MESH = pl.DeviceIdType.MESH
 VMEM = pl.BlockSpec(memory_space=pltpu.VMEM)
@@ -105,7 +105,9 @@
         arrived(g, 1, -1)
         arrived(g, 1, 1)
         arrived(g, 0, 2)
-        if g % 2 == 0:
+        if g in (2, 5):
+            send(g, 0, 2, "x", 6)
+        elif g % 2 == 0:
             send(g, 1, -1, "p", 6)
         else:
             send(g, 1, 1, "m", 6)
@@ -131,12 +133,20 @@
     loads[4].wait()
 
 
-def tile_kernel(slabs, blocks, col_ref, live_ref, gh_ref, tiles_ref, mid_ref, out_ref, acc):
+def tile_kernel(slabs, blocks, col_ref, live_ref, gh_ref, tiles_ref, mid_ref, out_ref, acc, term, rows):
     slots = tiles_ref.shape[1]
     window = (2 * REACH + 1) * blocks
     every = slabs * blocks
     first_row = (lax.axis_index("blk") - REACH) * blocks
     acc[...] = jnp.zeros_like(acc)
+    term[...] = jnp.zeros_like(term)
+    count = term.shape[0]
+    for t in range(count):
+        rows[t] = window
+
+    def settle():
+        for t in range(count):
+            acc[rows[t]] += term[t]
 
     def step(i, carry):
         pair = (2 * i, 2 * i + 1)
@@ -146,18 +156,22 @@
 
             @pl.when(half * (slots // 2) < most)
             def _(half=half):
+                settle()
+                t = 0
                 for k, b in enumerate(pair):
                     grad = gh_ref[b]
                     for s in range(half * (slots // 2), (half + 1) * (slots // 2)):
                         away = (col_ref[s, b] - first_row + every) & (every - 1)
-                        row = jnp.where(s < live[k], away, window)
-                        acc[row] += jnp.dot(
+                        rows[t] = jnp.where(s < live[k], away, window)
+                        term[t] = jnp.dot(
                             grad, tiles_ref[b, s], preferred_element_type=jnp.float32
                         )
+                        t += 1
 
         return carry
 
     lax.fori_loop(0, blocks // 2, step, 0)
+    settle()
     for w in range(2 * REACH + 1):
         part = acc[w * blocks : (w + 1) * blocks]
         if w == REACH:
@@ -182,7 +196,7 @@
     def across(bit):
         return me + bit - 2 * bit * ((me // bit) % 2)
 
-    bits = [1] + [bit for bit in (4, 8) if bit < slabs] + [2]
+    bits = [2, 1] + [bit for bit in (4, 8) if bit < slabs]
     partner = across(1)
     peers = [at(ahead), at(2 * ahead), at(-2 * ahead)] + [across(bit) for bit in bits]
     barrier = pltpu.get_barrier_semaphore()
@@ -211,15 +225,15 @@
     far_copy = copy(out_ref.at[far], far_in, k, at(2 * ahead))
     near_copy = copy(out_ref.at[back_near], near_in, k + 1, partner)
     k += 2
-    for one in helps:
-        one.start()
-    far_copy.start()
-    near_copy.start()
     weights = []
     for i, bit in enumerate(bits):
         src = wpart_ref if i == 0 else wsum.at[i - 1]
         weights.append(copy(src, wsum_in.at[i], k + i, across(bit)))
     weights[0].start()
+    for one in helps:
+        one.start()
+    far_copy.start()
+    near_copy.start()
     for p, c in enumerate(cuts):
         helps[p].wait_recv()
         both[c] = (
@@ -291,7 +305,11 @@
         ),
         in_specs=[SMEM, SMEM, VMEM, VMEM],
         out_specs=(VMEM, VMEM),
-        scratch_shapes=[pltpu.VMEM(((2 * REACH + 1) * blocks + 1, cols, size), f32)],
+        scratch_shapes=[
+            pltpu.VMEM(((2 * REACH + 1) * blocks + 1, cols, size), f32),
+            pltpu.VMEM((slots, cols, size), f32),
+            pltpu.SMEM((slots,), jnp.int32),
+        ],
         compiler_params=pltpu.CompilerParams(vmem_limit_bytes=12 << 20),
         name="tiles",
     )(col_block.T, live_count, grad_h, tiles_here)

time: 51.3 us -> 52.8 us (1.029)
  Pallas kernels: 49.1 us -> 50.6 us
    pallas_call x1, Pallas kernels: 17.8 us -> 19.8 us  [on_device(): pl.pallas_call(functools.partial(exchange_kernel, slabs, scale), out_shap...]
where the time goes in v3:
time: 52.8 us; the launch traced here: 52.7 us
  Pallas kernels  50.6 us (96%)
  local copies, waits for them, and re-layouts  1.33 us (3%)
  between operations  0.69 us (1%)
    pallas_call x1, Pallas kernels, on_device(): pl.pallas_call(functools.partial(gather_kernel, ring), out_shape=(jax.Sha...  21.6 us
    pallas_call x1, Pallas kernels, on_device(): pl.pallas_call(functools.partial(exchange_kernel, slabs, scale), out_shap...  19.8 us
    pallas_call x1, Pallas kernels, on_device(): pl.pallas_call(functools.partial(tile_kernel, slabs, blocks), out_shape=(...  9.24 us
    unnamed x6, local copies, waits for them, and re-layouts  1.33 us

profile of v3, /device:TPU:1, one launch (start us, length us, event | category | flops | bytes accessed | tf_op | source)
XLA Modules:
  0.0 52.7 jit_solution(12920414049155321294)
XLA Ops:
  0.6 0.0 copy-start.1
  0.6 0.0 copy-start
  0.7 21.6 %gather.1 = (bf16[32,32,128]{2,1,0:T(8,128)(2,1)S(1)}, f32[32,256]{1,0:T(8,128)S(1)}, bf16[32,16,128,128]{3,2,1,0:T(8,128)(2,1)S(1)}) custom-call(bf16[32,32,128]{2,1,0:T(8,128)(2,1)} %cot_hbm.1, s32[32,32,128]{2,1,0:T(8,128)} %mask_hbm.1, bf16[32,32,128]{2,1,0:T(8,128)(2,1)} %agg_hbm.1, bf16[32,256]{1,0:T(8,128)(2,1)} %w_hbm.1, ...), custom_call_target="tpu_custom_call" | custom-call | tf_op jit(solution)/shard_map/gather/pallas_call | solution.py:274
  22.3 0.0 copy-done.1
  22.3 0.0 copy-done
  22.3 9.2 %tiles.1 = (f32[32,32,128]{2,1,0:T(8,128)S(1)}, bf16[4,32,32,128]{3,2,1,0:T(8,128)(2,1)S(1)}) custom-call(s32[16,32]{1,0:T(8,128)S(1)} %bitcast.1, s32[32]{0:T(128)S(1)} %copy-done.1, bf16[32,32,128]{2,1,0:T(8,128)(2,1)S(1)} %get-tuple-element.7.gh_ref, bf16[32,16,128,128]{3,2,1,0:T(8,128)(2,1)S(1)} %get-tuple-element.8.tiles_ref), custom_call_target="tpu_custom_call" | custom-call | tf_op jit(solution)/shard_map/tiles/pallas_call | solution.py:300
  31.6 19.8 %exchange.1 = (bf16[32,32,128]{2,1,0:T(8,128)(2,1)S(1)}, f32[32,256]{1,0:T(8,128)S(1)}) custom-call(f32[32,32,128]{2,1,0:T(8,128)S(1)} %get-tuple-element.9.mid_ref, bf16[4,32,32,128]{3,2,1,0:T(8,128)(2,1)S(1)} %get-tuple-element.10.out_ref, f32[32,256]{1,0:T(8,128)S(1)} %get-tuple-element.11.wpart_ref), custom_call_target="tpu_custom_call" | custom-call | tf_op jit(solution)/shard_map/exchange/pallas_call | solution.py:321
  51.3 0.7 %copy.11 = bf16[32,32,128]{2,1,0:T(8,128)(2,1)} copy(bf16[32,32,128]{2,1,0:T(8,128)(2,1)S(1)} %get-tuple-element.14) | data formatting | bytes 524288
  52.0 0.6 %copy.12 = f32[32,256]{1,0:T(8,128)} copy(f32[32,256]{1,0:T(8,128)S(1)} %get-tuple-element.15) | data formatting | bytes 65536
Async XLA Ops:
  0.6 21.7 %copy-start.1 = (s32[32]{0:T(128)S(1)}, s32[32]{0:T(128)}, u32[]{:S(2)}) copy-start(s32[32]{0:T(128)} %live_ref.1) | copy-start | bytes 388
  0.6 21.7 %copy-start = (s32[32,16]{0,1:T(8,128)S(1)}, s32[32,16]{0,1:T(8,128)}, u32[]{:S(2)}) copy-start(s32[32,16]{0,1:T(8,128)} %param.12) | copy-start | bytes 6148

commit v4 on v3

--- a/solution.py
+++ b/solution.py
@@ -134,7 +134,8 @@
 
 
 def tile_kernel(slabs, blocks, col_ref, live_ref, gh_ref, tiles_ref, mid_ref, out_ref, acc, term, rows):
-    slots = tiles_ref.shape[1]
+    slots, size = tiles_ref.shape[1], tiles_ref.shape[3]
+    cols = gh_ref.shape[1]
     window = (2 * REACH + 1) * blocks
     every = slabs * blocks
     first_row = (lax.axis_index("blk") - REACH) * blocks
@@ -160,13 +161,14 @@
                 t = 0
                 for k, b in enumerate(pair):
                     grad = gh_ref[b]
-                    for s in range(half * (slots // 2), (half + 1) * (slots // 2)):
-                        away = (col_ref[s, b] - first_row + every) & (every - 1)
-                        rows[t] = jnp.where(s < live[k], away, window)
-                        term[t] = jnp.dot(
-                            grad, tiles_ref[b, s], preferred_element_type=jnp.float32
-                        )
-                        t += 1
+                    for s in range(half * (slots // 2), (half + 1) * (slots // 2), 2):
+                        both = jnp.concatenate([tiles_ref[b, s], tiles_ref[b, s + 1]], axis=1)
+                        terms = jnp.dot(grad, both, preferred_element_type=jnp.float32)
+                        for j in range(2):
+                            away = (col_ref[s + j, b] - first_row + every) & (every - 1)
+                            rows[t + j] = jnp.where(s + j < live[k], away, window)
+                            term[t + j] = terms[:, j * size : (j + 1) * size]
+                        t += 2
 
         return carry
 

time: 52.8 us -> 50.8 us (0.962); the launches traced: 52.7 us -> 49.9 us
  Pallas kernels: 50.6 us -> 47.9 us
    pallas_call x1, Pallas kernels: 9.24 us -> 5.44 us  [on_device(): pl.pallas_call(functools.partial(tile_kernel, slabs, blocks), out_shape=(...]
    pallas_call x1, Pallas kernels: 19.8 us -> 20.8 us  [on_device(): pl.pallas_call(functools.partial(exchange_kernel, slabs, scale), out_shap...]
where the time goes in v4:
time: 50.8 us; the launch traced here: 49.9 us
  Pallas kernels  47.9 us (94%)
  local copies, waits for them, and re-layouts  1.33 us (3%)
  between operations  0.68 us (1%)
    pallas_call x1, Pallas kernels, on_device(): pl.pallas_call(functools.partial(gather_kernel, ring), out_shape=(jax.Sha...  21.6 us
    pallas_call x1, Pallas kernels, on_device(): pl.pallas_call(functools.partial(exchange_kernel, slabs, scale), out_shap...  20.8 us
    pallas_call x1, Pallas kernels, on_device(): pl.pallas_call(functools.partial(tile_kernel, slabs, blocks), out_shape=(...  5.44 us
    unnamed x6, local copies, waits for them, and re-layouts  1.33 us

profile of v4, /device:TPU:1, one launch (start us, length us, event | category | flops | bytes accessed | tf_op | source)
XLA Modules:
  0.0 49.9 jit_solution(5435611585288376053)
XLA Ops:
  0.6 0.0 copy-start.1
  0.6 0.0 copy-start
  0.7 21.6 %gather.1 = (bf16[32,32,128]{2,1,0:T(8,128)(2,1)S(1)}, f32[32,256]{1,0:T(8,128)S(1)}, bf16[32,16,128,128]{3,2,1,0:T(8,128)(2,1)S(1)}) custom-call(bf16[32,32,128]{2,1,0:T(8,128)(2,1)} %cot_hbm.1, s32[32,32,128]{2,1,0:T(8,128)} %mask_hbm.1, bf16[32,32,128]{2,1,0:T(8,128)(2,1)} %agg_hbm.1, bf16[32,256]{1,0:T(8,128)(2,1)} %w_hbm.1, ...), custom_call_target="tpu_custom_call" | custom-call | tf_op jit(solution)/shard_map/gather/pallas_call | solution.py:276
  22.3 0.0 copy-done.1
  22.3 0.0 copy-done
  22.3 5.4 %tiles.1 = (f32[32,32,128]{2,1,0:T(8,128)S(1)}, bf16[4,32,32,128]{3,2,1,0:T(8,128)(2,1)S(1)}) custom-call(s32[16,32]{1,0:T(8,128)S(1)} %bitcast.1, s32[32]{0:T(128)S(1)} %copy-done.1, bf16[32,32,128]{2,1,0:T(8,128)(2,1)S(1)} %get-tuple-element.7.gh_ref, bf16[32,16,128,128]{3,2,1,0:T(8,128)(2,1)S(1)} %get-tuple-element.8.tiles_ref), custom_call_target="tpu_custom_call" | custom-call | tf_op jit(solution)/shard_map/tiles/pallas_call | solution.py:302
  27.8 20.8 %exchange.1 = (bf16[32,32,128]{2,1,0:T(8,128)(2,1)S(1)}, f32[32,256]{1,0:T(8,128)S(1)}) custom-call(f32[32,32,128]{2,1,0:T(8,128)S(1)} %get-tuple-element.9.mid_ref, bf16[4,32,32,128]{3,2,1,0:T(8,128)(2,1)S(1)} %get-tuple-element.10.out_ref, f32[32,256]{1,0:T(8,128)S(1)} %get-tuple-element.11.wpart_ref), custom_call_target="tpu_custom_call" | custom-call | tf_op jit(solution)/shard_map/exchange/pallas_call | solution.py:323
  48.5 0.7 %copy.11 = bf16[32,32,128]{2,1,0:T(8,128)(2,1)} copy(bf16[32,32,128]{2,1,0:T(8,128)(2,1)S(1)} %get-tuple-element.14) | data formatting | bytes 524288
  49.2 0.6 %copy.12 = f32[32,256]{1,0:T(8,128)} copy(f32[32,256]{1,0:T(8,128)S(1)} %get-tuple-element.15) | data formatting | bytes 65536
Async XLA Ops:
  0.6 21.7 %copy-start.1 = (s32[32]{0:T(128)S(1)}, s32[32]{0:T(128)}, u32[]{:S(2)}) copy-start(s32[32]{0:T(128)} %live_ref.1) | copy-start | bytes 388
  0.6 21.7 %copy-start = (s32[32,16]{0,1:T(8,128)S(1)}, s32[32,16]{0,1:T(8,128)}, u32[]{:S(2)}) copy-start(s32[32,16]{0,1:T(8,128)} %param.12) | copy-start | bytes 6148

commit v5 on v4

--- a/solution.py
+++ b/solution.py
@@ -89,7 +89,7 @@
     loads[4].start()
     loads[2].wait()
     loads[3].wait()
-    for g in range(GROUPS):
+    def first(g):
         arrived(g, 0, -1)
         arrived(g, 0, 1)
         arrived(g, 1, 0)
@@ -101,7 +101,8 @@
             send(g, 1, 0, "p", 3)
             send(g, 1, 0, "m", 4)
             send(g, 0, 1, "m", 5)
-    for g in range(GROUPS):
+
+    def second(g):
         arrived(g, 1, -1)
         arrived(g, 1, 1)
         arrived(g, 0, 2)
@@ -111,7 +112,8 @@
             send(g, 1, -1, "p", 6)
         else:
             send(g, 1, 1, "m", 6)
-    for g in range(GROUPS):
+
+    def finish(g):
         arrived(g, 1, 2)
 
         def step(i, carry):
@@ -127,6 +129,11 @@
             return carry
 
         lax.fori_loop(0, per // 4, step, 0)
+
+    for t in range(GROUPS + 4):
+        for work, late in ((first, 0), (second, 2), (finish, 4)):
+            if 0 <= t - late < GROUPS:
+                work(t - late)
     wpart_ref[...] = wacc[...]
     for one in sent:
         one.wait_send()

time: 50.8 us -> 55.9 us (1.10); the launches traced: 49.9 us -> 55.8 us
  Pallas kernels: 47.9 us -> 53.8 us
    pallas_call x1, Pallas kernels: 21.6 us -> 24.3 us  [on_device(): pl.pallas_call(functools.partial(gather_kernel, ring), out_shape=(jax.Sha...]
    pallas_call x1, Pallas kernels: 5.44 us -> 7.73 us  [on_device(): pl.pallas_call(functools.partial(tile_kernel, slabs, blocks), out_shape=(...]
    pallas_call x1, Pallas kernels: 20.8 us -> 21.7 us  [on_device(): pl.pallas_call(functools.partial(exchange_kernel, slabs, scale), out_shap...]
where the time goes in v5:
time: 55.9 us; the launch traced here: 55.8 us
  Pallas kernels  53.8 us (96%)
  local copies, waits for them, and re-layouts  1.33 us (2%)
  between operations  0.68 us (1%)
    pallas_call x1, Pallas kernels, on_device(): pl.pallas_call(functools.partial(gather_kernel, ring), out_shape=(jax.Sha...  24.3 us
    pallas_call x1, Pallas kernels, on_device(): pl.pallas_call(functools.partial(exchange_kernel, slabs, scale), out_shap...  21.7 us
    pallas_call x1, Pallas kernels, on_device(): pl.pallas_call(functools.partial(tile_kernel, slabs, blocks), out_shape=(...  7.73 us
    unnamed x6, local copies, waits for them, and re-layouts  1.33 us

profile of v5, /device:TPU:1, one launch (start us, length us, event | category | flops | bytes accessed | tf_op | source)
XLA Modules:
  0.0 55.8 jit_solution(3335958996196040605)
XLA Ops:
  0.6 0.0 copy-start.1
  0.6 0.0 copy-start
  0.7 24.3 %gather.1 = (bf16[32,32,128]{2,1,0:T(8,128)(2,1)S(1)}, f32[32,256]{1,0:T(8,128)S(1)}, bf16[32,16,128,128]{3,2,1,0:T(8,128)(2,1)S(1)}) custom-call(bf16[32,32,128]{2,1,0:T(8,128)(2,1)} %cot_hbm.1, s32[32,32,128]{2,1,0:T(8,128)} %mask_hbm.1, bf16[32,32,128]{2,1,0:T(8,128)(2,1)} %agg_hbm.1, bf16[32,256]{1,0:T(8,128)(2,1)} %w_hbm.1, ...), custom_call_target="tpu_custom_call" | custom-call | tf_op jit(solution)/shard_map/gather/pallas_call | solution.py:283
  25.0 0.0 copy-done.1
  25.0 0.0 copy-done
  25.0 7.7 %tiles.1 = (f32[32,32,128]{2,1,0:T(8,128)S(1)}, bf16[4,32,32,128]{3,2,1,0:T(8,128)(2,1)S(1)}) custom-call(s32[16,32]{1,0:T(8,128)S(1)} %bitcast.1, s32[32]{0:T(128)S(1)} %copy-done.1, bf16[32,32,128]{2,1,0:T(8,128)(2,1)S(1)} %get-tuple-element.7.gh_ref, bf16[32,16,128,128]{3,2,1,0:T(8,128)(2,1)S(1)} %get-tuple-element.8.tiles_ref), custom_call_target="tpu_custom_call" | custom-call | tf_op jit(solution)/shard_map/tiles/pallas_call | solution.py:309
  32.7 21.7 %exchange.1 = (bf16[32,32,128]{2,1,0:T(8,128)(2,1)S(1)}, f32[32,256]{1,0:T(8,128)S(1)}) custom-call(f32[32,32,128]{2,1,0:T(8,128)S(1)} %get-tuple-element.9.mid_ref, bf16[4,32,32,128]{3,2,1,0:T(8,128)(2,1)S(1)} %get-tuple-element.10.out_ref, f32[32,256]{1,0:T(8,128)S(1)} %get-tuple-element.11.wpart_ref), custom_call_target="tpu_custom_call" | custom-call | tf_op jit(solution)/shard_map/exchange/pallas_call | solution.py:330
  54.5 0.7 %copy.11 = bf16[32,32,128]{2,1,0:T(8,128)(2,1)} copy(bf16[32,32,128]{2,1,0:T(8,128)(2,1)S(1)} %get-tuple-element.14) | data formatting | bytes 524288
  55.2 0.6 %copy.12 = f32[32,256]{1,0:T(8,128)} copy(f32[32,256]{1,0:T(8,128)S(1)} %get-tuple-element.15) | data formatting | bytes 65536
Async XLA Ops:
  0.6 24.4 %copy-start.1 = (s32[32]{0:T(128)S(1)}, s32[32]{0:T(128)}, u32[]{:S(2)}) copy-start(s32[32]{0:T(128)} %live_ref.1) | copy-start | bytes 388
  0.6 24.4 %copy-start = (s32[32,16]{0,1:T(8,128)S(1)}, s32[32,16]{0,1:T(8,128)}, u32[]{:S(2)}) copy-start(s32[32,16]{0,1:T(8,128)} %param.12) | copy-start | bytes 6148
